TPU v7x, 32 devices: a whole 2x2x4 slice. The times are simulated.
32 devices in a mesh: ctx: 16 (over z, x, core), head: 2 (over y).
Axes of the slice: x: 2, y: 2, z: 4, core: 2. Of those that a mesh axis runs over, the one named last changes fastest.
Arguments:
- q_absorbed: bfloat16 [2048, 64, 576], P('ctx', 'head'), may hold values from -6 to 6
- grad_out: bfloat16 [2048, 64, 512], P('ctx', 'head'), may hold values from -6 to 6
- log_norm: float32 [2048, 64], P('ctx', 'head'), may hold values from 5 to 7
- out_dot: float32 [2048, 64], P('ctx', 'head'), may hold values from -6 to 6
- kv_cache: bfloat16 [2048, 576], P(('ctx', 'head')), may hold values from -6 to 6
- block_links: int32 [16, 4], P('ctx'), may hold values 0 or 1
Outputs:
- d_query: bfloat16 [2048, 64, 576], P('ctx', 'head')
- d_kv: bfloat16 [2048, 576], P(('ctx', 'head'))
All inputs are finite; a program needn't handle non-finite values. No bound on the sum of `block_links` on one device may be relied on, other than what follows from the above.
Results may differ from a plain program's by a relative error of at most 0.0061.
Values may be sent and summed in bfloat16 or wider, within the bound.
A program may use at most 128 MiB of HBM per device.

v0:
```python
import functools
import math

import jax
import jax.numpy as jnp
from jax import lax
from jax.experimental import pallas as pl
from jax.experimental.pallas import tpu as pltpu
from jax.sharding import PartitionSpec as P

offset_list = (0, 1, 2, 8)
F32 = jnp.float32
BF16 = jnp.bfloat16


def dot(a, b, ca, cb):
    return lax.dot_general(a, b, (((ca,), (cb,)), ((), ())), preferred_element_type=F32)


MESH = pl.DeviceIdType.MESH
FIRST, LAST = (0, 2), (2, 4)


def fused_kernel(
    n_ctx, n_head, links, kv_ref, q_hbm, g_hbm, ln_ref, od_ref,
    dqv, dkv_ref,
    qv, graw, gwide, gv, dsv, pbv, acc, kvbuf, away, yrecv, fwd, crecv,
    q_sem, g_sem, gs_s, gs_r, fw_s, fw_r, ry_s, ry_r, rc_s, rc_r,
):
    me = lax.axis_index("ctx")
    head = lax.axis_index("head")
    steps, group, feat, toks = qv.shape
    chunks, width, heads, lat = graw.shape
    cols = group * toks
    n_off, _, part, _ = kvbuf.shape
    blk = n_head * part
    scale = feat ** (-0.5)
    log2e = math.log2(math.e)

    def load_g(i):
        return pltpu.make_async_copy(g_hbm.at[pl.ds(i * width, width)], graw.at[i], g_sem.at[i])

    def load_q(i):
        return pltpu.make_async_copy(q_hbm.at[pl.ds(i * group, group)], qv.at[i], q_sem.at[i])

    def loop(count, body, start=0):
        def run(i, carry):
            body(i)
            return carry

        lax.fori_loop(start, count, run, 0)

    def at_ctx(by):
        return (lax.rem(me + by + n_ctx, n_ctx), head)

    def at_head(by):
        return (me, lax.rem(head + by + n_head, n_head))

    def send(src, dst, s_sem, r_sem, where):
        return pltpu.make_async_remote_copy(
            src_ref=src, dst_ref=dst, send_sem=s_sem, recv_sem=r_sem, device_id=where, device_id_type=MESH
        )

    loop(chunks, lambda i: load_g(i).start())

    away_by = sorted({by % n_ctx for o in offset_list[1:] for by in (o, -o)})
    barrier = pltpu.get_barrier_semaphore()
    for by in away_by:
        pl.semaphore_signal(barrier, inc=1, device_id=at_ctx(by), device_id_type=MESH)
    for j in range(1, n_head):
        pl.semaphore_signal(barrier, inc=1, device_id=at_head(j), device_id_type=MESH)
    pl.semaphore_wait(barrier, len(away_by) + n_head - 1)

    gather = [
        send(kv_ref, kvbuf.at[pos, 0], gs_s.at[pos - 1], gs_r.at[pos - 1], at_ctx(offset_list[pos]))
        for pos in range(1, n_off)
    ]
    spread = [
        [
            send(kv_ref if pos == 0 else kvbuf.at[pos, 0], kvbuf.at[pos, j],
                 fw_s.at[pos, j - 1], fw_r.at[pos, j - 1], at_head(-j))
            for j in range(1, n_head)
        ]
        for pos in range(n_off)
    ]
    for copy in [gather[0]] + gather[:0:-1]:
        copy.start()
    for copy in spread[0]:
        copy.start()
    loop(steps, lambda i: load_q(i).start())
    kvbuf[0, 0] = kv_ref[...]

    def relayout(i):
        load_g(i).wait()
        wide = graw[i].reshape(width * heads, lat).astype(F32)
        lanes = gwide.shape[2]
        for c in range(gwide.shape[0]):
            gwide[c] = wide[:, c * lanes : (c + 1) * lanes]
        for h in range(heads):
            for c in range(gwide.shape[0]):
                gv[h // group, h % group, pl.ds(i * width, width), c * lanes : (c + 1) * lanes] = gwide[
                    c, pl.ds(h, width, stride=heads), :
                ].astype(BF16)

    loop(chunks - 1, relayout)

    def scores(i, low, high):
        keys = kvbuf[low:high].reshape((high - low) * blk, feat)
        q = jnp.concatenate([qv[i, k] for k in range(group)], 1)
        g = gv[i].reshape(cols, lat)
        ln = jnp.concatenate([ln_ref[i, k : k + 1, :] for k in range(group)], 1) * log2e
        od = jnp.concatenate([od_ref[i, k : k + 1, :] for k in range(group)], 1)
        s = dot(keys, q, 1, 0)
        dp = dot(keys[:, :lat], g, 1, 1)
        ps, dss = [], []
        for pos in range(low, high):
            sl = slice((pos - low) * blk, (pos - low + 1) * blk)
            bias = jnp.where(links[0, pos] > 0, ln, 1e30)
            p = jnp.exp2(s[sl] * (scale * log2e) - bias)
            if offset_list[pos] == 0:
                key = lax.broadcasted_iota(jnp.int32, p.shape, 0) + head * part
                key = jnp.where(key >= blk, key - blk, key)
                tok = lax.rem(lax.broadcasted_iota(jnp.int32, p.shape, 1), toks)
                p = jnp.where(tok >= key, p, 0.0)
            ps.append(p.astype(BF16))
            dss.append((p * (dp[sl] - od) * scale).astype(BF16))
        return jnp.concatenate(ps, 0), jnp.concatenate(dss, 0), q, g

    def key_terms(pb, ds, q, g, low, high):
        rows = slice(low * blk, high * blk)
        dk = dot(ds, q, 1, 1)
        dv = dot(pb, g, 1, 0)
        acc[rows, :lat] += dk[:, :lat] + dv
        acc[rows, lat:] += dk[:, lat:]

    def across(low, high, slot):
        return [
            send(away.at[j - 1, low:high], yrecv.at[j - 1, low:high], ry_s.at[slot, j - 1],
                 ry_r.at[slot, j - 1], at_head(j))
            for j in range(1, n_head)
        ]

    def pack(low, high):
        for pos in range(low, high):
            for j in range(1, n_head):
                start = pos * blk + j * part
                away[j - 1, pos] = acc[start : start + part, :].astype(BF16)

    def folded(pos):
        total = acc[pos * blk : pos * blk + part, :]
        for j in range(1, n_head):
            total = total + yrecv[j - 1, pos].astype(F32)
        return total

    back = [
        send(fwd.at[pos - 1], crecv.at[pos - 1], rc_s.at[pos - 1], rc_r.at[pos - 1], at_ctx(-offset_list[pos]))
        for pos in range(1, n_off)
    ]

    acc[...] = jnp.zeros_like(acc)

    def onward(low, high):
        for pos in range(low, high):
            gather[pos - 1].wait_recv()
            for copy in spread[pos]:
                copy.start()

    def arrive(low, high):
        for pos in range(low, high):
            for copy in spread[pos]:
                copy.wait_recv()

    def first(i):
        load_q(i).wait()
        pb, ds, _, _ = scores(i, *FIRST)
        dsv[i, : FIRST[1] * blk, :] = ds
        pbv[i] = pb

    onward(1, FIRST[1])
    loop(chunks, relayout, chunks - 1)
    arrive(*FIRST)
    loop(steps // 2, first)
    onward(*LAST)
    loop(steps, first, steps // 2)
    arrive(*LAST)

    def second(i):
        pb, ds, q, g = scores(i, *LAST)
        dsv[i, LAST[0] * blk : LAST[1] * blk, :] = ds
        key_terms(pb, ds, q, g, *LAST)

    loop(steps, second)
    pack(*LAST)

    def third(i):
        q = jnp.concatenate([qv[i, k] for k in range(group)], 1)
        key_terms(pbv[i], dsv[i, : FIRST[1] * blk, :], q, gv[i].reshape(cols, lat), *FIRST)

    def fourth(i):
        keys = kvbuf[...].reshape(n_off * blk, feat)
        dq = dot(keys, dsv[i], 0, 0).astype(BF16)
        for k in range(group):
            dqv[i, k] = dq[:, k * toks : (k + 1) * toks]

    far, near = across(*LAST, 1), across(*FIRST, 0)
    for copy in far:
        copy.start()
    loop(steps, third)
    for copy in far:
        copy.wait_recv()
    for pos in range(*LAST):
        fwd[pos - 1] = folded(pos).astype(BF16)
    pack(*FIRST)
    for pos in range(*LAST):
        back[pos - 1].start()
    for copy in near:
        copy.start()
    loop(steps, fourth)
    for copy in near:
        copy.wait_recv()
    for pos in range(1, FIRST[1]):
        fwd[pos - 1] = folded(pos).astype(BF16)
    total = folded(0)
    for pos in range(1, FIRST[1]):
        back[pos - 1].start()
    for copy in gather + sum(spread, []) + far + near:
        copy.wait_send()
    for copy in back[::-1]:
        copy.wait()
    for pos in range(1, n_off):
        total = total + crecv[pos - 1].astype(F32)
    dkv_ref[...] = total.astype(BF16)


def fused(n_ctx, n_head, q, g, ln, od, kv, links, group=8, width=32):
    heads, feat, toks = q.shape
    lat = g.shape[2]
    part = kv.shape[0]
    n_off = len(offset_list)
    group = math.gcd(group, heads)
    width = math.gcd(width, toks)
    steps, chunks = heads // group, toks // width
    cols, keys = group * toks, n_off * n_head * part
    near = FIRST[1] * n_head * part
    dma = pltpu.SemaphoreType.DMA
    hbm = pl.BlockSpec(memory_space=pl.ANY)
    vmem = pl.BlockSpec(memory_space=pltpu.VMEM)
    return pl.pallas_call(
        functools.partial(fused_kernel, n_ctx, n_head),
        in_specs=[pl.BlockSpec(memory_space=pltpu.SMEM), vmem, hbm, hbm, vmem, vmem],
        out_specs=[vmem, vmem],
        out_shape=[
            pltpu.VMEM((steps, group, feat, toks), BF16),
            jax.ShapeDtypeStruct((part, feat), BF16),
        ],
        scratch_shapes=[
            pltpu.VMEM((steps, group, feat, toks), BF16),
            pltpu.VMEM((chunks, width, heads, lat), BF16),
            pltpu.VMEM((lat // 128, width * heads, 128), F32),
            pltpu.VMEM((steps, group, toks, lat), BF16),
            pltpu.VMEM((steps, keys, cols), BF16),
            pltpu.VMEM((steps, near, cols), BF16),
            pltpu.VMEM((keys, feat), F32),
            pltpu.VMEM((n_off, n_head, part, feat), BF16),
            pltpu.VMEM((n_head - 1, n_off, part, feat), BF16),
            pltpu.VMEM((n_head - 1, n_off, part, feat), BF16),
            pltpu.VMEM((n_off - 1, part, feat), BF16),
            pltpu.VMEM((n_off - 1, part, feat), BF16),
            dma((steps,)),
            dma((chunks,)),
            dma((n_off - 1,)),
            dma((n_off - 1,)),
            dma((n_off, n_head - 1)),
            dma((n_off, n_head - 1)),
            dma((2, n_head - 1)),
            dma((2, n_head - 1)),
            dma((n_off - 1,)),
            dma((n_off - 1,)),
        ],
        compiler_params=pltpu.CompilerParams(
            collective_id=0, has_side_effects=True, vmem_limit_bytes=67043328 - 2 * heads * feat * toks - 16384
        ),
        cost_estimate=pl.CostEstimate(flops=12 * 10**9, bytes_accessed=14 * 10**6, transcendentals=2 * 10**6),
        name="mla_bwd",
    )(links, kv, q, g, ln.reshape(steps, group, toks), od.reshape(steps, group, toks))


def shards(q, g, ln, od, kv, links):
    dq, dkv = fused(
        lax.axis_size("ctx"),
        lax.axis_size("head"),
        jnp.transpose(q, (1, 2, 0)),
        g,
        ln.T,
        od.T,
        kv,
        links,
    )
    return jnp.transpose(dq.reshape(-1, *dq.shape[2:]), (2, 0, 1)), dkv


def solution(mesh):
    in_specs = (
        P("ctx", "head", None),
        P("ctx", "head", None),
        P("ctx", "head"),
        P("ctx", "head"),
        P(("ctx", "head"), None),
        P("ctx", None),
    )
    out_specs = (P("ctx", "head", None), P(("ctx", "head"), None))
    return jax.shard_map(shards, mesh=mesh, in_specs=in_specs, out_specs=out_specs, check_vma=False)
```

profile of v0, /device:TPU:0, one launch (start us, length us, event | category | flops | bytes accessed | tf_op | source)
XLA Modules:
  0.0 44.0 jit_solution(10614576024629145587)
XLA Ops:
  0.6 40.5 %mla_bwd.1 = (bf16[4,8,576,128]{3,2,1,0:T(8,128)(2,1)S(1)}, bf16[64,576]{1,0:T(8,128)(2,1)}) custom-call(s32[1,4]{1,0:T(1,128)} %links.1, bf16[64,576]{1,0:T(8,128)(2,1)} %kv_ref.1, bf16[32,576,128]{2,1,0:T(8,128)(2,1)} %bitcast.11, bf16[128,32,512]{2,1,0:T(8,128)(2,1)} %g_hbm.1, f32[4,8,128]{2,1,0:T(8,128)} %bitcast.12, f32[4,8,128]{2,1,0:T(8,128)} %bitcast.13), custom_call_target="tpu_custom_call" | custom-call | flops 12000000000 | bytes 14000000 | tf_op jit(solution)/shard_map/mla_bwd/pallas_call | solution.py:248
  41.2 0.0 copy-start
  41.2 2.2 %copy.10 = bf16[128,32,576]{0,2,1:T(8,128)(2,1)} copy(bf16[128,32,576]{0,2,1:T(8,128)(2,1)S(1)} %bitcast.10) | data formatting | bytes 9437184
  43.4 0.0 copy-done
  43.4 0.6 %copy.11 = bf16[64,576]{1,0:T(8,128)(2,1)} copy(bf16[64,576]{1,0:T(8,128)(2,1)S(1)} %copy-done) | data formatting | bytes 147456
Async XLA Ops:
  41.2 2.2 %copy-start = (bf16[64,576]{1,0:T(8,128)(2,1)S(1)}, bf16[64,576]{1,0:T(8,128)(2,1)}, u32[]{:S(2)}) copy-start(bf16[64,576]{1,0:T(8,128)(2,1)} %get-tuple-element.11) | copy-start | bytes 221188
where the time goes:
time: 44.2 us; the launch traced here: 44 us
  Pallas kernels  40.5 us (92%)
  local copies, waits for them, and re-layouts  2.83 us (6%)
  between operations  0.65 us (1%)
    pallas_call x1, Pallas kernels, fused(): pl.pallas_call(functools.partial(fused_kernel, n_ctx, n_head), in_specs=[...  40.5 us
    unnamed x4, local copies, waits for them, and re-layouts  2.83 us

commit v1 on v0

v1 whole, which is shorter than its diff:
```python
import functools
import math

import jax
import jax.numpy as jnp
from jax import lax
from jax.experimental import pallas as pl
from jax.experimental.pallas import tpu as pltpu
from jax.sharding import PartitionSpec as P

offset_list = (0, 1, 2, 8)
F32 = jnp.float32
BF16 = jnp.bfloat16


def dot(a, b, ca, cb):
    return lax.dot_general(a, b, (((ca,), (cb,)), ((), ())), preferred_element_type=F32)


MESH = pl.DeviceIdType.MESH
FIRST, LAST = (0, 2), (2, 4)
TILE = 16


def fused_kernel(
    n_ctx, n_head, links, kv_hbm, q_hbm, g_hbm, ln_hbm, od_hbm,
    dqv, dkv_ref,
    qv, graw, perm, gv, ln_ref, od_ref, dsv, pbv, acc, kvbuf, away, yrecv, fwd, crecv, drecv,
    q_sem, g_sem, in_sem, gs_s, gs_r, fw_s, fw_r, ry_s, ry_r, rc_s, rc_r, rd_s, rd_r,
):
    me = lax.axis_index("ctx")
    head = lax.axis_index("head")
    steps, group, feat, toks = qv.shape
    chunks, width, heads, lat = graw.shape
    cols = group * toks
    n_off, _, part, _ = kvbuf.shape
    blk = n_head * part
    scale = feat ** (-0.5)
    log2e = math.log2(math.e)

    def load_g(i):
        return pltpu.make_async_copy(g_hbm.at[pl.ds(i * width, width)], graw.at[i], g_sem.at[i])

    def load_q(i):
        return pltpu.make_async_copy(q_hbm.at[pl.ds(i * group, group)], qv.at[i], q_sem.at[i])

    def loop(start, stop, body):
        def run(i, carry):
            body(i)
            return carry

        lax.fori_loop(start, stop, run, 0)

    def peer(by, j=0):
        return (lax.rem(me + by + n_ctx, n_ctx), lax.rem(head + j + n_head, n_head))

    def send(src, dst, s_sem, r_sem, where):
        return pltpu.make_async_remote_copy(
            src_ref=src, dst_ref=dst, send_sem=s_sem, recv_sem=r_sem, device_id=where, device_id_type=MESH
        )

    for i in range(chunks):
        load_g(i).start()
    own = pltpu.make_async_copy(kv_hbm, kvbuf.at[0, 0], in_sem.at[0])
    norms = pltpu.make_async_copy(ln_hbm, ln_ref, in_sem.at[1])
    dots = pltpu.make_async_copy(od_hbm, od_ref, in_sem.at[2])

    places = {(by % n_ctx, 0) for o in offset_list[1:] for by in (o, -o)}
    places |= {(by % n_ctx, j) for by in (offset_list[1], -offset_list[1]) for j in range(1, n_head)}
    places |= {(0, j) for j in range(1, n_head)}
    barrier = pltpu.get_barrier_semaphore()
    for by, j in sorted(places):
        pl.semaphore_signal(barrier, inc=1, device_id=peer(by, j), device_id_type=MESH)
    for copy in (own, norms, dots):
        copy.start()
    for i in range(steps):
        load_q(i).start()

    rows = perm.shape[0]
    out_row = lax.broadcasted_iota(jnp.int32, (rows, rows), 0)
    in_row = lax.broadcasted_iota(jnp.int32, (rows, rows), 1)
    in_head = lax.rem(in_row, heads)
    perm[...] = jnp.where(out_row * heads == in_head * (rows - 1) + in_row, 1.0, 0.0).astype(BF16)
    acc[...] = jnp.zeros_like(acc)

    gather = [
        send(kv_hbm, kvbuf.at[pos, 0], gs_s.at[pos - 1], gs_r.at[pos - 1], peer(offset_list[pos]))
        for pos in range(1, n_off)
    ]
    spread = [
        [
            send(kv_hbm if pos == 0 else kvbuf.at[pos, 0], kvbuf.at[pos, j],
                 fw_s.at[pos, j - 1], fw_r.at[pos, j - 1], peer(0, -j))
            for j in range(1, n_head)
        ]
        for pos in range(n_off)
    ]
    pl.semaphore_wait(barrier, len(places))
    for copy in spread[0]:
        copy.start()
    for copy in [gather[0]] + gather[:0:-1]:
        copy.start()

    def relayout(i):
        load_g(i).wait()
        size = rows // heads
        tile = max(TILE, size)
        for start in range(0, width, tile):
            parts = []
            for s in range(start, start + tile, size):
                block = graw[i, s : s + size].reshape(rows, lat)
                parts.append(dot(perm[...], block, 1, 0).reshape(heads, size, lat))
            moved = jnp.concatenate(parts, 1).astype(BF16)
            for h in range(heads):
                gv[h // group, h % group, pl.ds(pl.multiple_of(i * width + start, tile), tile), :] = moved[h]

    def scores(i, low, high):
        keys = kvbuf[low:high].reshape((high - low) * blk, feat)
        q = jnp.concatenate([qv[i, k] for k in range(group)], 1)
        g = gv[i].reshape(cols, lat)
        ln = jnp.concatenate([ln_ref[i, k : k + 1, :] for k in range(group)], 1) * log2e
        od = jnp.concatenate([od_ref[i, k : k + 1, :] for k in range(group)], 1)
        s = dot(keys, q, 1, 0)
        dp = dot(keys[:, :lat], g, 1, 1)
        ps, dss = [], []
        for pos in range(low, high):
            sl = slice((pos - low) * blk, (pos - low + 1) * blk)
            bias = jnp.where(links[0, pos] > 0, ln, 1e30)
            p = jnp.exp2(s[sl] * (scale * log2e) - bias)
            if offset_list[pos] == 0:
                key = lax.broadcasted_iota(jnp.int32, p.shape, 0) + head * part
                key = jnp.where(key >= blk, key - blk, key)
                tok = lax.rem(lax.broadcasted_iota(jnp.int32, p.shape, 1), toks)
                p = jnp.where(tok >= key, p, 0.0)
            ps.append(p.astype(BF16))
            dss.append((p * (dp[sl] - od) * scale).astype(BF16))
        return jnp.concatenate(ps, 0), jnp.concatenate(dss, 0), q, g

    def key_terms(pb, ds, q, g, low, high):
        span = slice(low * blk, high * blk)
        dk = dot(ds, q, 1, 1)
        dv = dot(pb, g, 1, 0)
        acc[span, :lat] += dk[:, :lat] + dv
        acc[span, lat:] += dk[:, lat:]

    def rows_of(pos, j):
        return acc[pos * blk + j * part : pos * blk + (j + 1) * part, :]

    across = [
        [
            send(away.at[j - 1, pos], yrecv.at[j - 1, pos], ry_s.at[pos, j - 1], ry_r.at[pos, j - 1], peer(0, j))
            for j in range(1, n_head)
        ]
        for pos in range(n_off)
    ]
    back = [
        send(fwd.at[pos - 1], crecv.at[pos - 1], rc_s.at[pos - 1], rc_r.at[pos - 1], peer(-offset_list[pos]))
        for pos in range(1, n_off)
    ]
    skew = [
        send(away.at[j - 1, 1], drecv.at[j - 1], rd_s.at[j - 1], rd_r.at[j - 1], peer(-offset_list[1], j))
        for j in range(1, n_head)
    ]

    def start(copies):
        for copy in copies:
            copy.start()

    def arrive(copies):
        for copy in copies:
            copy.wait_recv()

    def pack(pos):
        for j in range(1, n_head):
            away[j - 1, pos] = rows_of(pos, j).astype(BF16)

    def folded(pos):
        arrive(across[pos])
        total = rows_of(pos, 0)
        for j in range(1, n_head):
            total = total + yrecv[j - 1, pos].astype(F32)
        return total

    def first(i):
        pb, ds, _, _ = scores(i, *FIRST)
        dsv[i, : FIRST[1] * blk, :] = ds
        pbv[i] = pb

    def second(i):
        pb, ds, q, g = scores(i, *LAST)
        dsv[i, LAST[0] * blk : LAST[1] * blk, :] = ds
        key_terms(pb, ds, q, g, *LAST)

    def third(i):
        q = jnp.concatenate([qv[i, k] for k in range(group)], 1)
        key_terms(pbv[i], dsv[i, : FIRST[1] * blk, :], q, gv[i].reshape(cols, lat), *FIRST)

    def fourth(i):
        keys = kvbuf[...].reshape(n_off * blk, feat)
        dq = dot(keys, dsv[i], 0, 0).astype(BF16)
        for k in range(group):
            dqv[i, k] = dq[:, k * toks : (k + 1) * toks]

    loop(0, chunks, relayout)
    for copy in (own, norms, dots):
        copy.wait()
    for i in range(steps):
        load_q(i).wait()
    arrive([gather[0]])
    start(spread[1])
    arrive(spread[0] + spread[1])
    loop(0, steps // 2, first)
    for pos in range(*LAST)[::-1]:
        arrive([gather[pos - 1]])
        start(spread[pos])
    loop(steps // 2, steps, first)
    arrive(spread[2] + spread[3])
    loop(0, steps, second)
    for pos in range(*LAST)[::-1]:
        pack(pos)
        start(across[pos])
    loop(0, steps // 2, third)
    fwd[2] = folded(3).astype(BF16)
    start([back[2]])
    loop(steps // 2, steps, third)
    pack(1)
    fwd[0] = rows_of(1, 0).astype(BF16)
    start(skew + [back[0]])
    pack(0)
    start(across[0])
    fwd[1] = folded(2).astype(BF16)
    start([back[1]])
    loop(0, steps, fourth)
    total = folded(0)
    for copy in gather + sum(spread, []) + sum([across[p] for p in (0, 2, 3)], []):
        copy.wait_send()
    for copy in skew + back:
        copy.wait()
    for j in range(1, n_head):
        total = total + drecv[j - 1].astype(F32)
    for pos in range(1, n_off):
        total = total + crecv[pos - 1].astype(F32)
    dkv_ref[...] = total.astype(BF16)


def graw_rows(heads):
    return max(8, 256 // heads) * heads


def fused(n_ctx, n_head, q, g, ln, od, kv, links, group=8, width=32):
    heads, feat, toks = q.shape
    lat = g.shape[2]
    part = kv.shape[0]
    n_off = len(offset_list)
    group = math.gcd(group, heads)
    width = math.gcd(width, toks)
    steps, chunks = heads // group, toks // width
    cols, keys = group * toks, n_off * n_head * part
    near = FIRST[1] * n_head * part
    rows = graw_rows(heads)
    dma = pltpu.SemaphoreType.DMA
    hbm = pl.BlockSpec(memory_space=pl.ANY)
    vmem = pl.BlockSpec(memory_space=pltpu.VMEM)
    return pl.pallas_call(
        functools.partial(fused_kernel, n_ctx, n_head),
        in_specs=[pl.BlockSpec(memory_space=pltpu.SMEM), hbm, hbm, hbm, hbm, hbm],
        out_specs=[vmem, vmem],
        out_shape=[
            pltpu.VMEM((steps, group, feat, toks), BF16),
            jax.ShapeDtypeStruct((part, feat), BF16),
        ],
        scratch_shapes=[
            pltpu.VMEM((steps, group, feat, toks), BF16),
            pltpu.VMEM((chunks, width, heads, lat), BF16),
            pltpu.VMEM((rows, rows), BF16),
            pltpu.VMEM((steps, group, toks, lat), BF16),
            pltpu.VMEM((steps, group, toks), F32),
            pltpu.VMEM((steps, group, toks), F32),
            pltpu.VMEM((steps, keys, cols), BF16),
            pltpu.VMEM((steps, near, cols), BF16),
            pltpu.VMEM((keys, feat), F32),
            pltpu.VMEM((n_off, n_head, part, feat), BF16),
            pltpu.VMEM((n_head - 1, n_off, part, feat), BF16),
            pltpu.VMEM((n_head - 1, n_off, part, feat), BF16),
            pltpu.VMEM((n_off - 1, part, feat), BF16),
            pltpu.VMEM((n_off - 1, part, feat), BF16),
            pltpu.VMEM((n_head - 1, part, feat), BF16),
            dma((steps,)),
            dma((chunks,)),
            dma((3,)),
            dma((n_off - 1,)),
            dma((n_off - 1,)),
            dma((n_off, n_head - 1)),
            dma((n_off, n_head - 1)),
            dma((n_off, n_head - 1)),
            dma((n_off, n_head - 1)),
            dma((n_off - 1,)),
            dma((n_off - 1,)),
            dma((n_head - 1,)),
            dma((n_head - 1,)),
        ],
        compiler_params=pltpu.CompilerParams(
            collective_id=0, has_side_effects=True, vmem_limit_bytes=67043328 - 2 * heads * feat * toks - 16384
        ),
        cost_estimate=pl.CostEstimate(flops=12 * 10**9, bytes_accessed=14 * 10**6, transcendentals=2 * 10**6),
        name="mla_bwd",
    )(links, kv, q, g, ln.reshape(steps, group, toks), od.reshape(steps, group, toks))


def shards(q, g, ln, od, kv, links):
    dq, dkv = fused(
        lax.axis_size("ctx"),
        lax.axis_size("head"),
        jnp.transpose(q, (1, 2, 0)),
        g,
        ln.T,
        od.T,
        kv,
        links,
    )
    return jnp.transpose(dq.reshape(-1, *dq.shape[2:]), (2, 0, 1)), dkv


def solution(mesh):
    in_specs = (
        P("ctx", "head", None),
        P("ctx", "head", None),
        P("ctx", "head"),
        P("ctx", "head"),
        P(("ctx", "head"), None),
        P("ctx", None),
    )
    out_specs = (P("ctx", "head", None), P(("ctx", "head"), None))
    return jax.shard_map(shards, mesh=mesh, in_specs=in_specs, out_specs=out_specs, check_vma=False)
```

time: 44.2 us -> 41.4 us (0.937)
  Pallas kernels: 40.5 us -> 37.7 us
    pallas_call x1, Pallas kernels: 40.5 us -> 37.7 us  [fused(): pl.pallas_call(functools.partial(fused_kernel, n_ctx, n_head), in_specs=[...]
where the time goes in v1:
time: 41.4 us; the launch traced here: 41.2 us
  Pallas kernels  37.7 us (91%)
  local copies, waits for them, and re-layouts  2.83 us (7%)
  between operations  0.65 us (2%)
    pallas_call x1, Pallas kernels, fused(): pl.pallas_call(functools.partial(fused_kernel, n_ctx, n_head), in_specs=[...  37.7 us
    unnamed x4, local copies, waits for them, and re-layouts  2.83 us

profile of v1, /device:TPU:0, one launch (start us, length us, event | category | flops | bytes accessed | tf_op | source)
XLA Modules:
  0.0 41.2 jit_solution(10626643065079641050)
XLA Ops:
  0.6 37.7 %mla_bwd.1 = (bf16[4,8,576,128]{3,2,1,0:T(8,128)(2,1)S(1)}, bf16[64,576]{1,0:T(8,128)(2,1)}) custom-call(s32[1,4]{1,0:T(1,128)} %links.1, bf16[64,576]{1,0:T(8,128)(2,1)} %kv_hbm.1, bf16[32,576,128]{2,1,0:T(8,128)(2,1)} %bitcast.11, bf16[128,32,512]{2,1,0:T(8,128)(2,1)} %g_hbm.1, f32[4,8,128]{2,1,0:T(8,128)} %bitcast.12, f32[4,8,128]{2,1,0:T(8,128)} %bitcast.13), custom_call_target="tpu_custom_call" | custom-call | flops 12000000000 | bytes 14000000 | tf_op jit(solution)/shard_map/mla_bwd/pallas_call | solution.py:264
  38.4 0.0 copy-start
  38.4 2.2 %copy.10 = bf16[128,32,576]{0,2,1:T(8,128)(2,1)} copy(bf16[128,32,576]{0,2,1:T(8,128)(2,1)S(1)} %bitcast.10) | data formatting | bytes 9437184
  40.6 0.0 copy-done
  40.6 0.6 %copy.11 = bf16[64,576]{1,0:T(8,128)(2,1)} copy(bf16[64,576]{1,0:T(8,128)(2,1)S(1)} %copy-done) | data formatting | bytes 147456
Async XLA Ops:
  38.4 2.2 %copy-start = (bf16[64,576]{1,0:T(8,128)(2,1)S(1)}, bf16[64,576]{1,0:T(8,128)(2,1)}, u32[]{:S(2)}) copy-start(bf16[64,576]{1,0:T(8,128)(2,1)} %get-tuple-element.11) | copy-start | bytes 221188

commit v2 on v1

--- a/solution.py
+++ b/solution.py
@@ -8,7 +8,6 @@
 from jax.experimental.pallas import tpu as pltpu
 from jax.sharding import PartitionSpec as P
 
-offset_list = (0, 1, 2, 8)
 F32 = jnp.float32
 BF16 = jnp.bfloat16
 
@@ -18,8 +17,16 @@
 
 
 MESH = pl.DeviceIdType.MESH
-FIRST, LAST = (0, 2), (2, 4)
 TILE = 16
+GROUP = 8
+SLOTS = ((0, 0), (1, 1), (2, 2), (8, 3))
+GO = (2, 3)
+PLAN = (
+    ("have", 0), ("sckt", 0, 1, 0, 2), ("relay", 2), ("hop", 0), ("relay", 3), ("sckt", 0, 1, 2, 3),
+    ("have", 2), ("hop", 1), ("sckt", 0, 1, 3, 4), ("have", 3), ("sckt", 2, 4, 0, 4), ("fold", 3), ("fold", 2),
+    ("fold", 0), ("have", 1), ("sckt", 1, 2, 0, 2), ("pass", 3), ("sckt", 1, 2, 2, 3), ("pass", 2),
+    ("sckt", 1, 2, 3, 4), ("direct", 1), ("dq", 0, 4),
+)
 
 
 def fused_kernel(
@@ -49,7 +56,8 @@
             body(i)
             return carry
 
-        lax.fori_loop(start, stop, run, 0)
+        if stop > start:
+            lax.fori_loop(start, stop, run, 0)
 
     def peer(by, j=0):
         return (lax.rem(me + by + n_ctx, n_ctx), lax.rem(head + j + n_head, n_head))
@@ -65,11 +73,10 @@
     norms = pltpu.make_async_copy(ln_hbm, ln_ref, in_sem.at[1])
     dots = pltpu.make_async_copy(od_hbm, od_ref, in_sem.at[2])
 
-    places = {(by % n_ctx, 0) for o in offset_list[1:] for by in (o, -o)}
-    places |= {(by % n_ctx, j) for by in (offset_list[1], -offset_list[1]) for j in range(1, n_head)}
-    places |= {(0, j) for j in range(1, n_head)}
+    odd = lax.rem(me, 2)
+    places = [(-o, 0) for o, _ in SLOTS[2:]] + [(0, j) for j in range(1, n_head)] + [(1 - 2 * odd, 0)]
     barrier = pltpu.get_barrier_semaphore()
-    for by, j in sorted(places):
+    for by, j in places:
         pl.semaphore_signal(barrier, inc=1, device_id=peer(by, j), device_id_type=MESH)
     for copy in (own, norms, dots):
         copy.start()
@@ -84,7 +91,7 @@
     acc[...] = jnp.zeros_like(acc)
 
     gather = [
-        send(kv_hbm, kvbuf.at[pos, 0], gs_s.at[pos - 1], gs_r.at[pos - 1], peer(offset_list[pos]))
+        send(kv_hbm, kvbuf.at[pos, 0], gs_s.at[pos - 1], gs_r.at[pos - 1], peer(SLOTS[pos][0]))
         for pos in range(1, n_off)
     ]
     spread = [
@@ -96,10 +103,13 @@
         for pos in range(n_off)
     ]
     pl.semaphore_wait(barrier, len(places))
-    for copy in spread[0]:
+    for copy in [gather[p - 1] for p in GO] + spread[0]:
         copy.start()
-    for copy in [gather[0]] + gather[:0:-1]:
-        copy.start()
+    hops = [
+        send(kvbuf.at[2 * odd, j], kvbuf.at[1, j], gs_s.at[0] if j == 0 else fw_s.at[1, j - 1],
+             gs_r.at[0] if j == 0 else fw_r.at[1, j - 1], peer(1 - 2 * odd))
+        for j in range(n_head)
+    ]
 
     def relayout(i):
         load_g(i).wait()
@@ -125,9 +135,9 @@
         ps, dss = [], []
         for pos in range(low, high):
             sl = slice((pos - low) * blk, (pos - low + 1) * blk)
-            bias = jnp.where(links[0, pos] > 0, ln, 1e30)
+            bias = jnp.where(links[0, SLOTS[pos][1]] > 0, ln, 1e30)
             p = jnp.exp2(s[sl] * (scale * log2e) - bias)
-            if offset_list[pos] == 0:
+            if SLOTS[pos][0] == 0:
                 key = lax.broadcasted_iota(jnp.int32, p.shape, 0) + head * part
                 key = jnp.where(key >= blk, key - blk, key)
                 tok = lax.rem(lax.broadcasted_iota(jnp.int32, p.shape, 1), toks)
@@ -154,12 +164,16 @@
         for pos in range(n_off)
     ]
     back = [
-        send(fwd.at[pos - 1], crecv.at[pos - 1], rc_s.at[pos - 1], rc_r.at[pos - 1], peer(-offset_list[pos]))
+        send(fwd.at[pos - 1], crecv.at[pos - 1], rc_s.at[pos - 1], rc_r.at[pos - 1], peer(-SLOTS[pos][0]))
         for pos in range(1, n_off)
     ]
     skew = [
-        send(away.at[j - 1, 1], drecv.at[j - 1], rd_s.at[j - 1], rd_r.at[j - 1], peer(-offset_list[1], j))
-        for j in range(1, n_head)
+        [
+            send(away.at[j - 1, pos], drecv.at[pos - 1, j - 1], rd_s.at[pos - 1, j - 1], rd_r.at[pos - 1, j - 1],
+                 peer(-SLOTS[pos][0], j))
+            for j in range(1, n_head)
+        ]
+        for pos in range(1, n_off)
     ]
 
     def start(copies):
@@ -170,9 +184,26 @@
         for copy in copies:
             copy.wait_recv()
 
-    def pack(pos):
+    def relay(pos):
+        arrive([gather[pos - 1]])
+        start(spread[pos])
+
+    def have(pos):
+        arrive(hops if pos == 1 else spread[pos])
+
+    def hop(part):
+        if part == 0:
+            start(hops[:1])
+        else:
+            start(hops[1:])
+
+    def issue(pos):
+        start([gather[pos - 1]])
+
+    def fold(pos):
         for j in range(1, n_head):
             away[j - 1, pos] = rows_of(pos, j).astype(BF16)
+        start(across[pos])
 
     def folded(pos):
         arrive(across[pos])
@@ -181,63 +212,74 @@
             total = total + yrecv[j - 1, pos].astype(F32)
         return total
 
-    def first(i):
-        pb, ds, _, _ = scores(i, *FIRST)
-        dsv[i, : FIRST[1] * blk, :] = ds
-        pbv[i] = pb
-
-    def second(i):
-        pb, ds, q, g = scores(i, *LAST)
-        dsv[i, LAST[0] * blk : LAST[1] * blk, :] = ds
-        key_terms(pb, ds, q, g, *LAST)
-
-    def third(i):
-        q = jnp.concatenate([qv[i, k] for k in range(group)], 1)
-        key_terms(pbv[i], dsv[i, : FIRST[1] * blk, :], q, gv[i].reshape(cols, lat), *FIRST)
-
-    def fourth(i):
+    def onward(pos):
+        fwd[pos - 1] = folded(pos).astype(BF16)
+        start([back[pos - 1]])
+
+    def direct(pos):
+        for j in range(1, n_head):
+            away[j - 1, pos] = rows_of(pos, j).astype(BF16)
+        fwd[pos - 1] = rows_of(pos, 0).astype(BF16)
+        start(skew[pos - 1] + [back[pos - 1]])
+
+    def query(i):
+        return jnp.concatenate([qv[i, k] for k in range(group)], 1)
+
+    def sc(i, low, high):
+        pb, ds, _, _ = scores(i, low, high)
+        dsv[i, low * blk : high * blk, :] = ds
+        pbv[i, low * blk : high * blk, :] = pb
+
+    def sckt(i, low, high):
+        pb, ds, q, g = scores(i, low, high)
+        dsv[i, low * blk : high * blk, :] = ds
+        key_terms(pb, ds, q, g, low, high)
+
+    def kt(i, low, high):
+        span = slice(low * blk, high * blk)
+        key_terms(pbv[i, span, :], dsv[i, span, :], query(i), gv[i].reshape(cols, lat), low, high)
+
+    def dq(i):
         keys = kvbuf[...].reshape(n_off * blk, feat)
-        dq = dot(keys, dsv[i], 0, 0).astype(BF16)
+        out = dot(keys, dsv[i], 0, 0).astype(BF16)
         for k in range(group):
-            dqv[i, k] = dq[:, k * toks : (k + 1) * toks]
+            dqv[i, k] = out[:, k * toks : (k + 1) * toks]
+
+    def scaled(part):
+        return part * steps // 4
 
     loop(0, chunks, relayout)
     for copy in (own, norms, dots):
         copy.wait()
     for i in range(steps):
         load_q(i).wait()
-    arrive([gather[0]])
-    start(spread[1])
-    arrive(spread[0] + spread[1])
-    loop(0, steps // 2, first)
-    for pos in range(*LAST)[::-1]:
-        arrive([gather[pos - 1]])
-        start(spread[pos])
-    loop(steps // 2, steps, first)
-    arrive(spread[2] + spread[3])
-    loop(0, steps, second)
-    for pos in range(*LAST)[::-1]:
-        pack(pos)
-        start(across[pos])
-    loop(0, steps // 2, third)
-    fwd[2] = folded(3).astype(BF16)
-    start([back[2]])
-    loop(steps // 2, steps, third)
-    pack(1)
-    fwd[0] = rows_of(1, 0).astype(BF16)
-    start(skew + [back[0]])
-    pack(0)
-    start(across[0])
-    fwd[1] = folded(2).astype(BF16)
-    start([back[1]])
-    loop(0, steps, fourth)
+    calls = {"relay": relay, "have": have, "fold": fold, "pass": onward, "direct": direct, "hop": hop, "issue": issue}
+    loops = {"sc": sc, "kt": kt, "sckt": sckt}
+    sent, got = gather[1:] + spread[0] + sum(spread[2:], []) + hops, []
+    for name, *args in PLAN:
+        if name == "dq":
+            loop(scaled(args[0]), scaled(args[1]), dq)
+        elif name in loops:
+            low, high, first, last = args
+            loop(scaled(first), scaled(last), lambda i, name=name, low=low, high=high: loops[name](i, low, high))
+        else:
+            calls[name](*args)
+            pos = args[0]
+            if name == "fold":
+                sent += across[pos]
+            elif name == "pass":
+                sent, got = sent + [back[pos - 1]], got + [back[pos - 1]]
+            elif name == "direct":
+                both = skew[pos - 1] + [back[pos - 1]]
+                sent, got = sent + both, got + both
     total = folded(0)
-    for copy in gather + sum(spread, []) + sum([across[p] for p in (0, 2, 3)], []):
+    for copy in sent:
         copy.wait_send()
-    for copy in skew + back:
-        copy.wait()
-    for j in range(1, n_head):
-        total = total + drecv[j - 1].astype(F32)
+    arrive(got)
+    directs = [args[0] for name, *args in PLAN if name == "direct"]
+    for pos in directs:
+        for j in range(1, n_head):
+            total = total + drecv[pos - 1, j - 1].astype(F32)
     for pos in range(1, n_off):
         total = total + crecv[pos - 1].astype(F32)
     dkv_ref[...] = total.astype(BF16)
@@ -247,16 +289,15 @@
     return max(8, 256 // heads) * heads
 
 
-def fused(n_ctx, n_head, q, g, ln, od, kv, links, group=8, width=32):
+def fused(n_ctx, n_head, q, g, ln, od, kv, links, group=GROUP, width=32):
     heads, feat, toks = q.shape
     lat = g.shape[2]
     part = kv.shape[0]
-    n_off = len(offset_list)
+    n_off = len(SLOTS)
     group = math.gcd(group, heads)
     width = math.gcd(width, toks)
     steps, chunks = heads // group, toks // width
     cols, keys = group * toks, n_off * n_head * part
-    near = FIRST[1] * n_head * part
     rows = graw_rows(heads)
     dma = pltpu.SemaphoreType.DMA
     hbm = pl.BlockSpec(memory_space=pl.ANY)
@@ -277,14 +318,14 @@
             pltpu.VMEM((steps, group, toks), F32),
             pltpu.VMEM((steps, group, toks), F32),
             pltpu.VMEM((steps, keys, cols), BF16),
-            pltpu.VMEM((steps, near, cols), BF16),
+            pltpu.VMEM((steps, keys, cols), BF16),
             pltpu.VMEM((keys, feat), F32),
             pltpu.VMEM((n_off, n_head, part, feat), BF16),
             pltpu.VMEM((n_head - 1, n_off, part, feat), BF16),
             pltpu.VMEM((n_head - 1, n_off, part, feat), BF16),
             pltpu.VMEM((n_off - 1, part, feat), BF16),
             pltpu.VMEM((n_off - 1, part, feat), BF16),
-            pltpu.VMEM((n_head - 1, part, feat), BF16),
+            pltpu.VMEM((n_off - 1, n_head - 1, part, feat), BF16),
             dma((steps,)),
             dma((chunks,)),
             dma((3,)),
@@ -296,8 +337,8 @@
             dma((n_off, n_head - 1)),
             dma((n_off - 1,)),
             dma((n_off - 1,)),
-            dma((n_head - 1,)),
-            dma((n_head - 1,)),
+            dma((n_off - 1, n_head - 1)),
+            dma((n_off - 1, n_head - 1)),
         ],
         compiler_params=pltpu.CompilerParams(
             collective_id=0, has_side_effects=True, vmem_limit_bytes=67043328 - 2 * heads * feat * toks - 16384

time: 41.4 us -> 37.9 us (0.915)
  the two profiles are of different devices: /device:TPU:0 before, /device:TPU:1 now
where the time goes in v2:
time: 37.9 us; the launch traced here: 37.7 us
  Pallas kernels  34.3 us (91%)
  local copies, waits for them, and re-layouts  2.83 us (7%)
  between operations  0.65 us (2%)
    pallas_call x1, Pallas kernels, fused(): pl.pallas_call(functools.partial(fused_kernel, n_ctx, n_head), in_specs=[...  34.3 us
    unnamed x4, local copies, waits for them, and re-layouts  2.83 us

profile of v2, /device:TPU:1, one launch (start us, length us, event | category | flops | bytes accessed | tf_op | source)
XLA Modules:
  0.0 37.7 jit_solution(14158550026163001884)
XLA Ops:
  0.6 34.3 %mla_bwd.1 = (bf16[4,8,576,128]{3,2,1,0:T(8,128)(2,1)S(1)}, bf16[64,576]{1,0:T(8,128)(2,1)}) custom-call(s32[1,4]{1,0:T(1,128)} %links.1, bf16[64,576]{1,0:T(8,128)(2,1)} %kv_hbm.1, bf16[32,576,128]{2,1,0:T(8,128)(2,1)} %bitcast.11, bf16[128,32,512]{2,1,0:T(8,128)(2,1)} %g_hbm.1, f32[4,8,128]{2,1,0:T(8,128)} %bitcast.12, f32[4,8,128]{2,1,0:T(8,128)} %bitcast.13), custom_call_target="tpu_custom_call" | custom-call | flops 12000000000 | bytes 14000000 | tf_op jit(solution)/shard_map/mla_bwd/pallas_call | solution.py:305
  34.9 0.0 copy-start
  34.9 2.2 %copy.10 = bf16[128,32,576]{0,2,1:T(8,128)(2,1)} copy(bf16[128,32,576]{0,2,1:T(8,128)(2,1)S(1)} %bitcast.10) | data formatting | bytes 9437184
  37.1 0.0 copy-done
  37.1 0.6 %copy.11 = bf16[64,576]{1,0:T(8,128)(2,1)} copy(bf16[64,576]{1,0:T(8,128)(2,1)S(1)} %copy-done) | data formatting | bytes 147456
Async XLA Ops:
  34.9 2.2 %copy-start = (bf16[64,576]{1,0:T(8,128)(2,1)S(1)}, bf16[64,576]{1,0:T(8,128)(2,1)}, u32[]{:S(2)}) copy-start(bf16[64,576]{1,0:T(8,128)(2,1)} %get-tuple-element.11) | copy-start | bytes 221188

commit v3 on v2

--- a/solution.py
+++ b/solution.py
@@ -19,13 +19,15 @@
 MESH = pl.DeviceIdType.MESH
 TILE = 16
 GROUP = 8
+FLUSH = 1
+PAIRED = ((2, 4), 'dq', (0, 1), (1, 2))
 SLOTS = ((0, 0), (1, 1), (2, 2), (8, 3))
 GO = (2, 3)
 PLAN = (
     ("have", 0), ("sckt", 0, 1, 0, 2), ("relay", 2), ("hop", 0), ("relay", 3), ("sckt", 0, 1, 2, 3),
-    ("have", 2), ("hop", 1), ("sckt", 0, 1, 3, 4), ("have", 3), ("sckt", 2, 4, 0, 4), ("fold", 3), ("fold", 2),
-    ("fold", 0), ("have", 1), ("sckt", 1, 2, 0, 2), ("pass", 3), ("sckt", 1, 2, 2, 3), ("pass", 2),
-    ("sckt", 1, 2, 3, 4), ("direct", 1), ("dq", 0, 4),
+    ("have", 2), ("hop", 1), ("sckt", 0, 1, 3, 4), ("have", 3), ("sckt", 2, 4, 0, 4), ("fold", 3),
+    ("fold", 2), ("have", 1), ("sckt", 1, 2, 0, 2), ("pass", 3), ("sckt", 1, 2, 2, 3), ("pass", 2),
+    ("sckt", 1, 2, 3, 4), ("direct", 1), ("fold", 0), ("dq", 0, 4),
 )
 
 
@@ -58,6 +60,18 @@
 
         if stop > start:
             lax.fori_loop(start, stop, run, 0)
+
+    def pairs(start, stop, body):
+        whole = start + (stop - start) // 2 * 2
+
+        def run(i, carry):
+            body(start + 2 * i)
+            body(start + 2 * i + 1)
+            return carry
+
+        if whole > start:
+            lax.fori_loop(0, (whole - start) // 2, run, 0)
+        loop(whole, stop, body)
 
     def peer(by, j=0):
         return (lax.rem(me + by + n_ctx, n_ctx), lax.rem(head + j + n_head, n_head))
@@ -258,10 +272,10 @@
     sent, got = gather[1:] + spread[0] + sum(spread[2:], []) + hops, []
     for name, *args in PLAN:
         if name == "dq":
-            loop(scaled(args[0]), scaled(args[1]), dq)
+            (pairs if 'dq' in PAIRED else loop)(scaled(args[0]), scaled(args[1]), dq)
         elif name in loops:
             low, high, first, last = args
-            loop(scaled(first), scaled(last), lambda i, name=name, low=low, high=high: loops[name](i, low, high))
+            (pairs if (low, high) in PAIRED else loop)(scaled(first), scaled(last), lambda i, name=name, low=low, high=high: loops[name](i, low, high))
         else:
             calls[name](*args)
             pos = args[0]
@@ -289,6 +303,19 @@
     return max(8, 256 // heads) * heads
 
 
+def flush_kernel(dq_ref, dkv_ref, dq_hbm, dkv_hbm, sem):
+    steps, group = dq_ref.shape[:2]
+    size = group // FLUSH
+    copies = [pltpu.make_async_copy(dkv_ref, dkv_hbm, sem.at[steps * FLUSH])]
+    for i in range(steps * FLUSH):
+        cut = (i // FLUSH, pl.ds(i % FLUSH * size, size))
+        copies.append(pltpu.make_async_copy(dq_ref.at[cut], dq_hbm.at[cut], sem.at[i]))
+    for copy in copies:
+        copy.start()
+    for copy in copies:
+        copy.wait()
+
+
 def fused(n_ctx, n_head, q, g, ln, od, kv, links, group=GROUP, width=32):
     heads, feat, toks = q.shape
     lat = g.shape[2]
@@ -302,13 +329,13 @@
     dma = pltpu.SemaphoreType.DMA
     hbm = pl.BlockSpec(memory_space=pl.ANY)
     vmem = pl.BlockSpec(memory_space=pltpu.VMEM)
-    return pl.pallas_call(
+    grads = pl.pallas_call(
         functools.partial(fused_kernel, n_ctx, n_head),
         in_specs=[pl.BlockSpec(memory_space=pltpu.SMEM), hbm, hbm, hbm, hbm, hbm],
         out_specs=[vmem, vmem],
         out_shape=[
             pltpu.VMEM((steps, group, feat, toks), BF16),
-            jax.ShapeDtypeStruct((part, feat), BF16),
+            pltpu.VMEM((part, feat), BF16),
         ],
         scratch_shapes=[
             pltpu.VMEM((steps, group, feat, toks), BF16),
@@ -341,11 +368,24 @@
             dma((n_off - 1, n_head - 1)),
         ],
         compiler_params=pltpu.CompilerParams(
-            collective_id=0, has_side_effects=True, vmem_limit_bytes=67043328 - 2 * heads * feat * toks - 16384
+            collective_id=0, has_side_effects=True, vmem_limit_bytes=67043328 - 2 * heads * feat * toks - 4 * part * (feat + 128) - (1 << 18)
         ),
         cost_estimate=pl.CostEstimate(flops=12 * 10**9, bytes_accessed=14 * 10**6, transcendentals=2 * 10**6),
         name="mla_bwd",
     )(links, kv, q, g, ln.reshape(steps, group, toks), od.reshape(steps, group, toks))
+    return pl.pallas_call(
+        flush_kernel,
+        in_specs=[vmem, vmem],
+        out_specs=[hbm, hbm],
+        out_shape=[
+            jax.ShapeDtypeStruct((steps, group, feat, toks), BF16),
+            jax.ShapeDtypeStruct((part, feat), BF16),
+        ],
+        scratch_shapes=[dma((steps * FLUSH + 1,))],
+        compiler_params=pltpu.CompilerParams(has_side_effects=True, vmem_limit_bytes=1 << 17),
+        cost_estimate=pl.CostEstimate(flops=0, bytes_accessed=10**7, transcendentals=0),
+        name="flush",
+    )(*[pltpu.with_memory_space_constraint(x, pltpu.VMEM) for x in grads])
 
 
 def shards(q, g, ln, od, kv, links):

time: 37.9 us -> 35.7 us (0.942)
  local copies, waits for them, and re-layouts: 2.83 us -> 0 us
  Pallas kernels: 34.3 us -> 34.9 us
    unnamed x4 -> x0, local copies, waits for them, and re-layouts: 2.83 us -> none
    pallas_call x0 -> x1, Pallas kernels: none -> 2.25 us  [fused(): pl.pallas_call(flush_kernel, in_specs=[vmem, vmem], out_specs=[hbm, hbm],...]
    pallas_call x1, Pallas kernels: 34.3 us -> 32.6 us  [fused(): pl.pallas_call(functools.partial(fused_kernel, n_ctx, n_head), in_specs=[...]
where the time goes in v3:
time: 35.7 us; the launch traced here: 35.5 us
  Pallas kernels  34.9 us (98%)
  between operations  0.64 us (2%)
    pallas_call x1, Pallas kernels, fused(): pl.pallas_call(functools.partial(fused_kernel, n_ctx, n_head), in_specs=[...  32.6 us
    pallas_call x1, Pallas kernels, fused(): pl.pallas_call(flush_kernel, in_specs=[vmem, vmem], out_specs=[hbm, hbm],...  2.25 us

profile of v3, /device:TPU:1, one launch (start us, length us, event | category | flops | bytes accessed | tf_op | source)
XLA Modules:
  0.0 35.5 jit_solution(16304596028946278340)
XLA Ops:
  0.6 32.6 %mla_bwd.1 = (bf16[4,8,576,128]{3,2,1,0:T(8,128)(2,1)S(1)}, bf16[64,576]{1,0:T(8,128)(2,1)S(1)}) custom-call(s32[1,4]{1,0:T(1,128)} %links.1, bf16[64,576]{1,0:T(8,128)(2,1)} %kv_hbm.1, bf16[32,576,128]{2,1,0:T(8,128)(2,1)} %bitcast.10, bf16[128,32,512]{2,1,0:T(8,128)(2,1)} %g_hbm.1, f32[4,8,128]{2,1,0:T(8,128)} %bitcast.12, f32[4,8,128]{2,1,0:T(8,128)} %bitcast.13), custom_call_target="tpu_custom_call" | custom-call | flops 12000000000 | bytes 14000000 | tf_op jit(solution)/shard_map/mla_bwd/pallas_call | solution.py:332
  33.2 2.2 %flush.1 = (bf16[4,8,576,128]{3,2,1,0:T(8,128)(2,1)}, bf16[64,576]{1,0:T(8,128)(2,1)}) custom-call(bf16[4,8,576,128]{3,2,1,0:T(8,128)(2,1)S(1)} %get-tuple-element.6.dq_ref, bf16[64,576]{1,0:T(8,128)(2,1)S(1)} %get-tuple-element.7.dkv_ref), custom_call_target="tpu_custom_call" | custom-call | bytes 10000000 | tf_op jit(solution)/shard_map/flush/pallas_call | solution.py:376

commit v4 on v3

--- a/solution.py
+++ b/solution.py
@@ -24,17 +24,17 @@
 SLOTS = ((0, 0), (1, 1), (2, 2), (8, 3))
 GO = (2, 3)
 PLAN = (
-    ("have", 0), ("sckt", 0, 1, 0, 2), ("relay", 2), ("hop", 0), ("relay", 3), ("sckt", 0, 1, 2, 3),
-    ("have", 2), ("hop", 1), ("sckt", 0, 1, 3, 4), ("have", 3), ("sckt", 2, 4, 0, 4), ("fold", 3),
-    ("fold", 2), ("have", 1), ("sckt", 1, 2, 0, 2), ("pass", 3), ("sckt", 1, 2, 2, 3), ("pass", 2),
-    ("sckt", 1, 2, 3, 4), ("direct", 1), ("fold", 0), ("dq", 0, 4),
+    ("have", 0), ("sckt", 0, 1, 0, 2), ("relay", 2), ("hop", 0), ("relay", 3), ("sckt", 0, 1, 2, 4),
+    ("have", 2), ("hop", 1), ("have", 3), ("sckt", 2, 4, 0, 4), ("fold", 3), ("fold", 2), ("have", 1),
+    ("sckt", 1, 2, 0, 3), ("pass", 3), ("pass", 2), ("sckt", 1, 2, 3, 4), ("direct", 1), ("fold", 0),
+    ("dq", 0, 4),
 )
 
 
 def fused_kernel(
-    n_ctx, n_head, links, kv_hbm, q_hbm, g_hbm, ln_hbm, od_hbm,
+    n_ctx, n_head, links_hbm, kv_hbm, q_hbm, g_hbm, ln_hbm, od_hbm,
     dqv, dkv_ref,
-    qv, graw, perm, gv, ln_ref, od_ref, dsv, pbv, acc, kvbuf, away, yrecv, fwd, crecv, drecv,
+    links, qv, graw, perm, gv, ln_ref, od_ref, dsv, pbv, acc, kvbuf, away, yrecv, fwd, crecv, drecv,
     q_sem, g_sem, in_sem, gs_s, gs_r, fw_s, fw_r, ry_s, ry_r, rc_s, rc_r, rd_s, rd_r,
 ):
     me = lax.axis_index("ctx")
@@ -81,9 +81,8 @@
             src_ref=src, dst_ref=dst, send_sem=s_sem, recv_sem=r_sem, device_id=where, device_id_type=MESH
         )
 
-    for i in range(chunks):
-        load_g(i).start()
     own = pltpu.make_async_copy(kv_hbm, kvbuf.at[0, 0], in_sem.at[0])
+    live = pltpu.make_async_copy(links_hbm, links, in_sem.at[3])
     norms = pltpu.make_async_copy(ln_hbm, ln_ref, in_sem.at[1])
     dots = pltpu.make_async_copy(od_hbm, od_ref, in_sem.at[2])
 
@@ -92,7 +91,9 @@
     barrier = pltpu.get_barrier_semaphore()
     for by, j in places:
         pl.semaphore_signal(barrier, inc=1, device_id=peer(by, j), device_id_type=MESH)
-    for copy in (own, norms, dots):
+    for i in range(chunks):
+        load_g(i).start()
+    for copy in (own, live, norms, dots):
         copy.start()
     for i in range(steps):
         load_q(i).start()
@@ -263,7 +264,7 @@
         return part * steps // 4
 
     loop(0, chunks, relayout)
-    for copy in (own, norms, dots):
+    for copy in (own, live, norms, dots):
         copy.wait()
     for i in range(steps):
         load_q(i).wait()
@@ -331,13 +332,14 @@
     vmem = pl.BlockSpec(memory_space=pltpu.VMEM)
     grads = pl.pallas_call(
         functools.partial(fused_kernel, n_ctx, n_head),
-        in_specs=[pl.BlockSpec(memory_space=pltpu.SMEM), hbm, hbm, hbm, hbm, hbm],
+        in_specs=[hbm] * 6,
         out_specs=[vmem, vmem],
         out_shape=[
             pltpu.VMEM((steps, group, feat, toks), BF16),
             pltpu.VMEM((part, feat), BF16),
         ],
         scratch_shapes=[
+            pltpu.SMEM(links.shape, jnp.int32),
             pltpu.VMEM((steps, group, feat, toks), BF16),
             pltpu.VMEM((chunks, width, heads, lat), BF16),
             pltpu.VMEM((rows, rows), BF16),
@@ -355,7 +357,7 @@
             pltpu.VMEM((n_off - 1, n_head - 1, part, feat), BF16),
             dma((steps,)),
             dma((chunks,)),
-            dma((3,)),
+            dma((4,)),
             dma((n_off - 1,)),
             dma((n_off - 1,)),
             dma((n_off, n_head - 1)),

time: 35.7 us -> 34.4 us (0.964)
  Pallas kernels: 34.9 us -> 33.4 us
    pallas_call x1, Pallas kernels: 32.6 us -> 31.2 us  [fused(): pl.pallas_call(functools.partial(fused_kernel, n_ctx, n_head), in_specs=[...]
where the time goes in v4:
time: 34.4 us; the launch traced here: 34.1 us
  Pallas kernels  33.4 us (97%)
  between operations  0.64 us (2%)
    pallas_call x1, Pallas kernels, fused(): pl.pallas_call(functools.partial(fused_kernel, n_ctx, n_head), in_specs=[...  31.2 us
    pallas_call x1, Pallas kernels, fused(): pl.pallas_call(flush_kernel, in_specs=[vmem, vmem], out_specs=[hbm, hbm],...  2.25 us

profile of v4, /device:TPU:1, one launch (start us, length us, event | category | flops | bytes accessed | tf_op | source)
XLA Modules:
  0.0 34.1 jit_solution(15069406601582529449)
XLA Ops:
  0.6 31.2 %mla_bwd.1 = (bf16[4,8,576,128]{3,2,1,0:T(8,128)(2,1)S(1)}, bf16[64,576]{1,0:T(8,128)(2,1)S(1)}) custom-call(s32[1,4]{1,0:T(1,128)} %links_hbm.1, bf16[64,576]{1,0:T(8,128)(2,1)} %kv_hbm.1, bf16[32,576,128]{2,1,0:T(8,128)(2,1)} %bitcast.10, bf16[128,32,512]{2,1,0:T(8,128)(2,1)} %g_hbm.1, f32[4,8,128]{2,1,0:T(8,128)} %bitcast.12, f32[4,8,128]{2,1,0:T(8,128)} %bitcast.13), custom_call_target="tpu_custom_call" | custom-call | flops 12000000000 | bytes 14000000 | tf_op jit(solution)/shard_map/mla_bwd/pallas_call | solution.py:333
  31.8 2.2 %flush.1 = (bf16[4,8,576,128]{3,2,1,0:T(8,128)(2,1)}, bf16[64,576]{1,0:T(8,128)(2,1)}) custom-call(bf16[4,8,576,128]{3,2,1,0:T(8,128)(2,1)S(1)} %get-tuple-element.6.dq_ref, bf16[64,576]{1,0:T(8,128)(2,1)S(1)} %get-tuple-element.7.dkv_ref), custom_call_target="tpu_custom_call" | custom-call | bytes 10000000 | tf_op jit(solution)/shard_map/flush/pallas_call | solution.py:378

commit v5 on v4

--- a/solution.py
+++ b/solution.py
@@ -25,9 +25,8 @@
 GO = (2, 3)
 PLAN = (
     ("have", 0), ("sckt", 0, 1, 0, 2), ("relay", 2), ("hop", 0), ("relay", 3), ("sckt", 0, 1, 2, 4),
-    ("have", 2), ("hop", 1), ("have", 3), ("sckt", 2, 4, 0, 4), ("fold", 3), ("fold", 2), ("have", 1),
-    ("sckt", 1, 2, 0, 3), ("pass", 3), ("pass", 2), ("sckt", 1, 2, 3, 4), ("direct", 1), ("fold", 0),
-    ("dq", 0, 4),
+    ("have", 2), ("hop", 1), ("have", 3), ("sckt", 2, 4, 0, 4), ("direct", 2), ("fold", 3), ("have", 1),
+    ("sckt", 1, 2, 0, 4), ("pass", 3), ("direct", 1), ("fold", 0), ("dq", 0, 4),
 )
 
 

time: 34.4 us -> 34.5 us (level)
  no operation moved by 1% of the time
where the time goes in v5:
time: 34.5 us; the launch traced here: 33.9 us
  Pallas kernels  33.3 us (97%)
  between operations  0.64 us (2%)
    pallas_call x1, Pallas kernels, fused(): pl.pallas_call(functools.partial(fused_kernel, n_ctx, n_head), in_specs=[...  31 us
    pallas_call x1, Pallas kernels, fused(): pl.pallas_call(flush_kernel, in_specs=[vmem, vmem], out_specs=[hbm, hbm],...  2.25 us

profile of v5, /device:TPU:1, one launch (start us, length us, event | category | flops | bytes accessed | tf_op | source)
XLA Modules:
  0.0 33.9 jit_solution(13250176424438203396)
XLA Ops:
  0.6 31.0 %mla_bwd.1 = (bf16[4,8,576,128]{3,2,1,0:T(8,128)(2,1)S(1)}, bf16[64,576]{1,0:T(8,128)(2,1)S(1)}) custom-call(s32[1,4]{1,0:T(1,128)} %links_hbm.1, bf16[64,576]{1,0:T(8,128)(2,1)} %kv_hbm.1, bf16[32,576,128]{2,1,0:T(8,128)(2,1)} %bitcast.10, bf16[128,32,512]{2,1,0:T(8,128)(2,1)} %g_hbm.1, f32[4,8,128]{2,1,0:T(8,128)} %bitcast.12, f32[4,8,128]{2,1,0:T(8,128)} %bitcast.13), custom_call_target="tpu_custom_call" | custom-call | flops 12000000000 | bytes 14000000 | tf_op jit(solution)/shard_map/mla_bwd/pallas_call | solution.py:332
  31.7 2.2 %flush.1 = (bf16[4,8,576,128]{3,2,1,0:T(8,128)(2,1)}, bf16[64,576]{1,0:T(8,128)(2,1)}) custom-call(bf16[4,8,576,128]{3,2,1,0:T(8,128)(2,1)S(1)} %get-tuple-element.6.dq_ref, bf16[64,576]{1,0:T(8,128)(2,1)S(1)} %get-tuple-element.7.dkv_ref), custom_call_target="tpu_custom_call" | custom-call | bytes 10000000 | tf_op jit(solution)/shard_map/flush/pallas_call | solution.py:377
